TPU v7x, 32 devices: a whole 2x2x4 slice. The times are simulated.
32 devices in a mesh: grp: 2 (over y), ia: 4 (over x, core), ja: 4 (over z).
Axes of the slice: x: 2, y: 2, z: 4, core: 2. Of those that a mesh axis runs over, the one named last changes fastest.
Arguments:
- amplitudes: float32 [16, 8, 160, 160], P(('grp', 'ia'), 'ja'), parts along dimension 0, may hold values from -3 to 3
- integrals: float32 [16, 8, 160, 160], P(('grp', 'ia'), 'ja'), parts along dimension 0, may hold values from -6 to 6
- row_intersection: float32 [16, 8, 8, 160, 160], P(('grp', 'ia'), 'ja'), parts along dimension 0, as said below
- column_intersection: float32 [16, 8, 8, 160, 160], P(('grp', 'ia'), 'ja'), parts along dimension 0, as said below
- row_tiles: int32 [16, 8], P(('grp', 'ia')), parts along dimension 0, may hold values from 0 to 7, as said below
- row_coupling: float32 [16, 8], P(('grp', 'ia')), parts along dimension 0, may hold values from 0.02 to 0.12
- row_counts: int32 [16], P(('grp', 'ia')), parts along dimension 0, may hold values from 1 to 8, as said below
- column_tiles: int32 [16, 8], P(('grp', 'ja')), parts along dimension 0, may hold values from 0 to 7, as said below
- column_coupling: float32 [16, 8], P(('grp', 'ja')), parts along dimension 0, may hold values from 0.02 to 0.12
- column_counts: int32 [16], P(('grp', 'ja')), parts along dimension 0, may hold values from 1 to 8, as said below
- virtual_energy: float32 [16, 8, 160], P(('grp', 'ia'), 'ja'), parts along dimension 0, may hold values from 0.5 to 3
- first_energy: float32 [16], P(('grp', 'ia')), parts along dimension 0, may hold values from -1.5 to -0.3
- second_energy: float32 [16], P(('grp', 'ja')), parts along dimension 0, may hold values from -1.5 to -0.3
Outputs:
- new_amplitudes: float32 [16, 8, 160, 160], P(('grp', 'ia'), 'ja'), parts along dimension 0
- last_residual: float32 [16, 8, 160, 160], P(('grp', 'ia'), 'ja'), parts along dimension 0
There are 2 independent parts, one for each index of `grp`. A program takes and returns all parts, laid end to end along the dimension named above; each array names one. Nothing has to cross between parts.
Inputs may be any that keep to these rules, and one draw needn't show every extreme that they name: `row_tiles`: each row holds 8 different first-fragment orbitals. `column_tiles`: each row holds 8 different second-fragment orbitals. `row_counts`: some orbital has all 8 slots live. `column_counts`: some orbital has all 8 slots live. `row_intersection`: identity plus an independent perturbation of full rank. `column_intersection`: identity plus an independent perturbation of full rank.
All inputs are finite; a program needn't handle non-finite values.
Results may differ from a plain program's by a relative error of at most 0.00017.
Values sent between devices are 32-bit elements; how exact they have to be, the bound alone decides.
No kernel may reach another device: no remote copies, remote signals or barrier semaphores. Data moves between devices by JAX's collectives and lax.ppermute only.
A program may use at most 128 MiB of HBM per device.

v0:
```python
import jax
import jax.numpy as jnp
from jax import lax
from jax.sharding import PartitionSpec as P

ITERS = 2


def sandwich(intersection, block):
    left = jnp.matmul(intersection, block, precision=lax.Precision.HIGHEST)
    return jnp.matmul(left, jnp.swapaxes(intersection, -1, -2), precision=lax.Precision.HIGHEST)


def coupled_sum(intersection, chosen, weight, counts, row_side):
    longest = jnp.max(counts)

    def one_slot(slot, total):
        over_slot = lax.dynamic_index_in_dim(intersection, slot, 2, keepdims=False)
        chosen_slot = lax.dynamic_index_in_dim(chosen, slot, 2, keepdims=False)
        weight_slot = lax.dynamic_index_in_dim(weight, slot, 1, keepdims=False)
        product = sandwich(over_slot, chosen_slot)
        if row_side:
            scaled = weight_slot[:, None, None, None] * product
        else:
            scaled = weight_slot[None, :, None, None] * product
        return total + scaled

    start = jnp.zeros(chosen.shape[:2] + chosen.shape[3:], jnp.float32)
    return lax.fori_loop(0, longest, one_slot, start)


def local(
    amplitudes,
    integrals,
    row_intersection,
    column_intersection,
    row_tiles,
    row_coupling,
    row_counts,
    column_tiles,
    column_coupling,
    column_counts,
    virtual_energy,
    first_energy,
    second_energy,
):
    denom = (
        virtual_energy[:, :, :, None]
        + virtual_energy[:, :, None, :]
        - first_energy[:, None, None, None]
        - second_energy[None, :, None, None]
    )
    slot_index = jnp.arange(row_tiles.shape[1], dtype=jnp.int32)
    row_weight = row_coupling * (slot_index[None, :] < row_counts[:, None]).astype(jnp.float32)
    column_weight = column_coupling * (slot_index[None, :] < column_counts[:, None]).astype(
        jnp.float32
    )
    current = amplitudes
    residual = jnp.zeros_like(amplitudes)
    for iteration in range(ITERS):
        gathered_rows = lax.all_gather(current, "ia", axis=0, tiled=True)
        gathered_columns = lax.all_gather(current, "ja", axis=1, tiled=True)
        row_chosen = jnp.swapaxes(gathered_rows[row_tiles], 1, 2)
        column_chosen = gathered_columns[:, column_tiles]
        row_term = coupled_sum(row_intersection, row_chosen, row_weight, row_counts, True)
        column_term = coupled_sum(
            column_intersection, column_chosen, column_weight, column_counts, False
        )
        residual = integrals + denom * current - row_term - column_term
        current = current - residual / denom
    return (current, residual)


def solution(mesh):
    placed = (
        P(("grp", "ia"), "ja", None, None),
        P(("grp", "ia"), "ja", None, None),
        P(("grp", "ia"), "ja", None, None, None),
        P(("grp", "ia"), "ja", None, None, None),
        P(("grp", "ia"), None),
        P(("grp", "ia"), None),
        P(("grp", "ia")),
        P(("grp", "ja"), None),
        P(("grp", "ja"), None),
        P(("grp", "ja")),
        P(("grp", "ia"), "ja", None),
        P(("grp", "ia")),
        P(("grp", "ja")),
    )
    return jax.shard_map(
        local,
        mesh=mesh,
        in_specs=placed,
        out_specs=(P(("grp", "ia"), "ja", None, None), P(("grp", "ia"), "ja", None, None)),
        check_vma=False,
    )
```

profile of v0, /device:TPU:16, one launch (start us, length us, event | category | flops | bytes accessed | tf_op | source)
XLA Modules:
  0.0 275.3 jit_solution(13624956626482143141)
XLA Ops:
  9.5 5.4 %copy.44 = f32[2,2,8,160,160]{4,3,1,0,2:T(8,128)} copy(f32[2,2,8,160,160]{4,3,2,1,0:T(8,128)} %param.23) | data formatting | bytes 6553600 | tf_op jit(solution)/shard_map/while | solution.py:29
  15.1 5.6 %copy.47 = f32[2,2,8,160,160]{4,3,1,0,2:T(8,128)} copy(f32[2,2,8,160,160]{4,3,2,1,0:T(8,128)} %param.24) | data formatting | bytes 6553600 | tf_op jit(solution)/shard_map/while | solution.py:29
  22.1 14.0 %all-gather.5.cloned.1.call-done = f32[8,2,160,160]{3,2,1,0:T(8,128)} async-done(((f32[2,2,160,160]{3,2,1,0:T(8,128)}), f32[8,2,160,160]{3,2,1,0:T(8,128)}) %all-gather.5.cloned.1.call-update) | async-done | bytes 1638416 | tf_op jit(solution)/shard_map/all_gather | solution.py:61
  36.2 5.0 %gather_fusion = f32[16,2,160,160]{3,2,1,0:T(8,128)} fusion(f32[8,2,160,160]{3,2,1,0:T(8,128)} %all-gather.5.cloned.1.call-done, s32[1024]{0:T(1024)S(1)} %pad_clamp_fusion.1), kind=kCustom, calls=%fused_computation | custom fusion | bytes 6553664 | tf_op jit(solution)/shard_map/gather | solution.py:63
  41.2 34.7 %while.40 = (s32[]{:T(128)}, f32[2,2,160,160]{3,2,1,0:T(8,128)S(1)}, s32[]{:T(128)}, f32[2,8]{0,1:T(8,128)S(1)}, f32[2,2,8,160,160]{4,3,1,0,2:T(8,128)}, /*index...) while((s32[]{:T(128)}, f32[2,2,160,160]{3,2,1,0:T(8,128)S(1)}, s32[]{:T(128)}, ...), condition=%wide.region_2.3_spmd, body=%wide.region_1.2_spmd.sunk | while | flops 393420800 | bytes 3605663 | solution.py:29
  44.0 2.1 fusion.81
  46.8 2.1 fusion.79
  56.5 2.1 fusion.79
  63.5 2.1 fusion.81
  71.1 2.1 fusion.79
  75.9 15.4 %all-gather.7.cloned.1.call-done = f32[2,8,160,160]{3,2,1,0:T(8,128)} async-done(((f32[2,2,160,160]{3,2,1,0:T(8,128)}), f32[2,8,160,160]{3,2,1,0:T(8,128)}) %all-gather.7.cloned.1.call-update) | async-done | bytes 1638416 | tf_op jit(solution)/shard_map/all_gather | solution.py:62
  91.3 5.0 %gather_fusion.1 = f32[16,2,160,160]{3,2,1,0:T(8,128)} fusion(f32[2,8,160,160]{3,2,1,0:T(8,128)} %all-gather.7.cloned.1.call-done, s32[1024]{0:T(1024)S(1)} %pad_clamp_fusion), kind=kCustom, calls=%fused_computation.1 | custom fusion | bytes 6553664 | tf_op jit(solution)/shard_map/gather | solution.py:64
  96.4 39.2 %while.41 = (s32[]{:T(128)}, f32[2,2,160,160]{3,2,1,0:T(8,128)S(1)}, s32[]{:T(128)}, f32[2,8]{0,1:T(8,128)S(1)}, f32[2,2,8,160,160]{4,3,1,0,2:T(8,128)}, /*index...) while((s32[]{:T(128)}, f32[2,2,160,160]{3,2,1,0:T(8,128)S(1)}, s32[]{:T(128)}, ...), condition=%wide.region_5.6_spmd, body=%wide.region_4.5_spmd.sunk | while | flops 393420800 | bytes 3605663 | solution.py:29
  137.3 25.0 %all-gather.9.cloned.1.call-done = f32[8,2,160,160]{3,2,1,0:T(8,128)} async-done(((f32[2,2,160,160]{3,2,1,0:T(8,128)}), f32[8,2,160,160]{3,2,1,0:T(8,128)}) %all-gather.9.cloned.1.call-update) | async-done | bytes 1638416 | tf_op jit(solution)/shard_map/all_gather | solution.py:61
  162.3 4.9 %gather_fusion.2 = f32[16,2,160,160]{3,2,1,0:T(8,128)} fusion(f32[8,2,160,160]{3,2,1,0:T(8,128)} %all-gather.9.cloned.1.call-done, s32[1024]{0:T(1024)S(1)} %pad_clamp_fusion.1), kind=kCustom, calls=%fused_computation.2 | custom fusion | bytes 6553664 | tf_op jit(solution)/shard_map/gather | solution.py:63
  167.2 5.4 %copy.60 = f32[2,8,2,160,160]{4,3,2,0,1:T(8,128)} copy(f32[2,8,2,160,160]{4,3,2,1,0:T(8,128)} %bitcast.100) | data formatting | bytes 6553600 | tf_op jit(solution)/shard_map/gather | solution.py:63
  172.6 34.7 %while.42 = (s32[]{:T(128)}, f32[2,2,160,160]{3,2,1,0:T(8,128)S(1)}, s32[]{:T(128)}, f32[2,8]{0,1:T(8,128)S(1)}, f32[2,2,8,160,160]{4,3,1,0,2:T(8,128)}, /*index...) while((s32[]{:T(128)}, f32[2,2,160,160]{3,2,1,0:T(8,128)S(1)}, s32[]{:T(128)}, ...), condition=%wide.region_7.8_spmd, body=%wide.region_6.7_spmd.sunk | while | flops 393420800 | bytes 3605663 | solution.py:29
  173.3 2.1 fusion.92
  183.1 2.1 fusion.92
  197.6 2.1 fusion.92
  207.3 10.6 %all-gather.11.cloned.1.call-done = f32[2,8,160,160]{3,2,1,0:T(8,128)} async-done(((f32[2,2,160,160]{3,2,1,0:T(8,128)}), f32[2,8,160,160]{3,2,1,0:T(8,128)}) %all-gather.11.cloned.1.call-update) | async-done | bytes 1638416 | tf_op jit(solution)/shard_map/all_gather | solution.py:62
  217.9 5.0 %gather_fusion.3 = f32[16,2,160,160]{3,2,1,0:T(8,128)} fusion(f32[2,8,160,160]{3,2,1,0:T(8,128)} %all-gather.11.cloned.1.call-done, s32[1024]{0:T(1024)S(1)} %pad_clamp_fusion), kind=kCustom, calls=%fused_computation.3 | custom fusion | bytes 6553664 | tf_op jit(solution)/shard_map/gather | solution.py:64
  222.8 5.4 %copy.59 = f32[2,8,2,160,160]{4,3,0,2,1:T(8,128)} copy(f32[2,8,2,160,160]{4,3,2,1,0:T(8,128)} %bitcast.101) | data formatting | bytes 6553600 | tf_op jit(solution)/shard_map/gather | solution.py:64
  228.3 39.1 %while.43 = (s32[]{:T(128)}, f32[2,2,160,160]{3,2,1,0:T(8,128)S(1)}, s32[]{:T(128)}, f32[2,8]{0,1:T(8,128)S(1)}, f32[2,2,8,160,160]{4,3,1,0,2:T(8,128)}, /*index...) while((s32[]{:T(128)}, f32[2,2,160,160]{3,2,1,0:T(8,128)S(1)}, s32[]{:T(128)}, ...), condition=%wide.region_9.10_spmd, body=%wide.region_8.9_spmd.sunk | while | flops 393420800 | bytes 3605663 | solution.py:29
  (130 shorter events, 114.2 us)
Async XLA Ops:
  7.2 29.0 %all-gather.5.cloned.1.call-start = ((), (), s32[]{:S(2)}) async-start(), calls=%async_computation | async-start | bytes 3276800 | tf_op jit(solution)/shard_map/all_gather | solution.py:61
  7.9 83.4 %all-gather.7.cloned.1.call-start = ((), (), s32[]{:S(2)}) async-start(), calls=%async_computation.1 | async-start | bytes 3276800 | tf_op jit(solution)/shard_map/all_gather | solution.py:62
  8.6 153.7 %all-gather.9.cloned.1.call-start = ((), (), s32[]{:S(2)}) async-start(), calls=%async_computation.2 | async-start | bytes 3276800 | tf_op jit(solution)/shard_map/all_gather | solution.py:61
  9.5 5.4 %copy-start.6 = (f32[2,8]{1,0:T(2,128)S(1)}, f32[2,8]{1,0:T(2,128)}, u32[]{:S(2)}) copy-start(f32[2,8]{1,0:T(2,128)} %param.26) | copy-start | bytes 196
  9.5 5.5 %copy-start.8 = (s32[2,8]{1,0:T(2,128)S(1)}, s32[2,8]{1,0:T(2,128)}, u32[]{:S(2)}) copy-start(s32[2,8]{1,0:T(2,128)} %param.28) | copy-start | bytes 196
  15.1 5.6 %copy-start.7 = (f32[2,8]{1,0:T(2,128)S(1)}, f32[2,8]{1,0:T(2,128)}, u32[]{:S(2)}) copy-start(f32[2,8]{1,0:T(2,128)} %param.29) | copy-start | bytes 196
  15.1 5.7 %copy-start.9 = (s32[2]{0:T(128)S(1)}, s32[2]{0:T(128)}, u32[]{:S(2)}) copy-start(s32[2]{0:T(128)} %param.27) | copy-start | bytes 28
  15.1 6.4 %copy-start.10 = (s32[2]{0:T(128)S(1)}, s32[2]{0:T(128)}, u32[]{:S(2)}) copy-start(s32[2]{0:T(128)} %param.30) | copy-start | bytes 28
  96.3 39.2 %copy-start.1 = (f32[2,2,160,160]{3,2,1,0:T(8,128)S(1)}, f32[2,2,160,160]{3,2,1,0:T(8,128)}, u32[]{:S(2)}) copy-start(f32[2,2,160,160]{3,2,1,0:T(8,128)} %param.21) | copy-start | bytes 1228804
  96.3 39.2 %copy-start.2 = (f32[2,2,160,160]{3,2,1,0:T(8,128)S(1)}, f32[2,2,160,160]{3,2,1,0:T(8,128)}, u32[]{:S(2)}) copy-start(f32[2,2,160,160]{3,2,1,0:T(8,128)} %param.22) | copy-start | bytes 1228804
  96.3 39.2 %copy-start.3 = (f32[2,2,160]{2,1,0:T(2,128)S(1)}, f32[2,2,160]{2,1,0:T(2,128)}, u32[]{:S(2)}) copy-start(f32[2,2,160]{2,1,0:T(2,128)} %param.31) | copy-start | bytes 7684
  96.4 39.2 %copy-start.4 = (f32[2]{0:T(128)S(1)}, f32[2]{0:T(128)}, u32[]{:S(2)}) copy-start(f32[2]{0:T(128)} %param.33) | copy-start | bytes 28
  96.4 39.2 %copy-start.5 = (f32[2]{0:T(128)S(1)}, f32[2]{0:T(128)}, u32[]{:S(2)}) copy-start(f32[2]{0:T(128)} %param.32) | copy-start | bytes 28
  136.8 81.1 %all-gather.11.cloned.1.call-start = ((), (), s32[]{:S(2)}) async-start(), calls=%async_computation.3 | async-start | bytes 3276800 | tf_op jit(solution)/shard_map/all_gather | solution.py:62
  228.3 39.2 %copy-start = (f32[2,2,160,160]{3,2,1,0:T(8,128)S(1)}, f32[2,2,160,160]{3,2,1,0:T(8,128)}, u32[]{:S(2)}) copy-start(f32[2,2,160,160]{3,2,1,0:T(8,128)} %divide_subtract_fusion.1) | copy-start | bytes 1228804
Sparse Core Ops, SparseCore 0:
  9.5 26.5 all-gather.4
  37.7 53.5 all-gather.6
  136.9 25.3 all-gather.8
  164.3 53.5 all-gather.10
where the time goes:
time: 278 us; the launch traced here: 275 us
  matrix products  123 us (44%)
  waiting for transfers between devices  66.9 us (24%)
  local copies, waits for them, and re-layouts  42.4 us (15%)
  loops' own time  24 us (9%)
  between operations  14 us (5%)
  other arithmetic  4.52 us (2%)
    dot_general x30, matrix products, sandwich(): left = jnp.matmul(intersection, block, precision=lax.Precision.HIGHEST)  61.7 us
    dot_general x30, matrix products, sandwich(): jnp.matmul(left, jnp.swapaxes(intersection, -1, -2), precision=lax.Precis...  61.7 us
    all_gather x2, waiting for transfers between devices, local(): gathered_rows = lax.all_gather(current, 'ia', axis=0, tiled=True)  39 us
    all_gather x2, waiting for transfers between devices, local(): gathered_columns = lax.all_gather(current, 'ja', axis=1, tiled=True)  26 us
    another operation x4, loops' own time, coupled_sum(): return lax.fori_loop(0, longest, one_slot, start)  24 us
    gather x3, local copies, waits for them, and re-layouts, local(): column_chosen = gathered_columns[:, column_tiles]  15.3 us
    gather x3, local copies, waits for them, and re-layouts, local(): row_chosen = jnp.swapaxes(gathered_rows[row_tiles], 1, 2)  15.2 us
    while x2, local copies, waits for them, and re-layouts, coupled_sum(): return lax.fori_loop(0, longest, one_slot, start)  11 us
  transfers between devices with their start and end apart: 4, of which 4 were waited for; matrix products, arithmetic and copies ran while one was open for 31% of the time, Pallas kernels for 0%

commit v1 on v0

--- a/solution.py
+++ b/solution.py
@@ -59,7 +59,15 @@
     residual = jnp.zeros_like(amplitudes)
     for iteration in range(ITERS):
         gathered_rows = lax.all_gather(current, "ia", axis=0, tiled=True)
-        gathered_columns = lax.all_gather(current, "ja", axis=1, tiled=True)
+        ways, here, step = (lax.axis_size("ja"), lax.axis_index("ja"), current.shape[1])
+        line, have = (current, 1)
+        while have < ways:
+            line = jnp.concatenate(
+                [line, lax.ppermute(line, "ja", [(d, (d - have) % ways) for d in range(ways)])],
+                axis=1,
+            )
+            have = 2 * have
+        gathered_columns = jnp.roll(line, here * step, axis=1)
         row_chosen = jnp.swapaxes(gathered_rows[row_tiles], 1, 2)
         column_chosen = gathered_columns[:, column_tiles]
         row_term = coupled_sum(row_intersection, row_chosen, row_weight, row_counts, True)

time: 278 us -> 348 us (1.25)
  the two profiles are of different devices: /device:TPU:16 before, /device:TPU:19 now
where the time goes in v1:
time: 348 us; the launch traced here: 345 us
  matrix products  131 us (38%)
  waiting for transfers between devices  116 us (33%)
  local copies, waits for them, and re-layouts  41 us (12%)
  loops' own time  26.3 us (8%)
  between operations  14.3 us (4%)
  other arithmetic  14 us (4%)
    ppermute x4, waiting for transfers between devices, local(): lax.ppermute(line, 'ja', [(d, (d - have) % ways) for d in range(ways)])  116 us
    dot_general x32, matrix products, sandwich(): jnp.matmul(left, jnp.swapaxes(intersection, -1, -2), precision=lax.Precis...  65.7 us
    dot_general x32, matrix products, sandwich(): left = jnp.matmul(intersection, block, precision=lax.Precision.HIGHEST)  65.6 us
    another operation x4, loops' own time, coupled_sum(): return lax.fori_loop(0, longest, one_slot, start)  26.3 us
    gather x3, local copies, waits for them, and re-layouts, local(): row_chosen = jnp.swapaxes(gathered_rows[row_tiles], 1, 2)  15.3 us
    gather x3, local copies, waits for them, and re-layouts, local(): column_chosen = gathered_columns[:, column_tiles]  11.8 us
    while x2, local copies, waits for them, and re-layouts, coupled_sum(): return lax.fori_loop(0, longest, one_slot, start)  10.8 us
  transfers between devices with their start and end apart: 6, of which 4 were waited for; matrix products, arithmetic and copies ran while one was open for 30% of the time, Pallas kernels for 0%

profile of v1, /device:TPU:19, one launch (start us, length us, event | category | flops | bytes accessed | tf_op | source)
XLA Modules:
  0.0 344.9 jit_solution(16708857341460478957)
XLA Ops:
  7.9 15.2 %collective-permute-done = f32[2,2,160,160]{3,2,1,0:T(8,128)S(1)} collective-permute-done((f32[2,2,160,160]{3,2,1,0:T(8,128)}, f32[2,2,160,160]{3,2,1,0:T(8,128)S(1)}, u32[]{:S(2)}, u32[]{:S(2)}) %collective-permute-start) | collective-permute-done | bytes 409632 | tf_op jit(solution)/shard_map/ppermute | solution.py:66
  32.2 5.4 %copy.47 = f32[2,2,8,160,160]{4,3,1,0,2:T(8,128)} copy(f32[2,2,8,160,160]{4,3,2,1,0:T(8,128)} %param.26) | data formatting | bytes 6553600 | tf_op jit(solution)/shard_map/while | solution.py:29
  37.7 5.4 %copy.44 = f32[2,2,8,160,160]{4,3,1,0,2:T(8,128)} copy(f32[2,2,8,160,160]{4,3,2,1,0:T(8,128)} %param.25) | data formatting | bytes 6553600 | tf_op jit(solution)/shard_map/while | solution.py:29
  43.1 37.8 %collective-permute-done.1 = f32[2,4,160,160]{3,2,1,0:T(8,128)} collective-permute-done((f32[2,4,160,160]{3,2,1,0:T(8,128)S(1)}, f32[2,4,160,160]{3,2,1,0:T(8,128)}, u32[]{:S(2)}, u32[]{:S(2)}) %collective-permute-start.1) | collective-permute-done | bytes 819232 | tf_op jit(solution)/shard_map/ppermute | solution.py:66
  80.9 3.0 fusion.49
  83.9 3.2 gather_fusion.1
  87.2 39.4 %while.41 = (s32[]{:T(128)}, f32[2,2,160,160]{3,2,1,0:T(8,128)S(1)}, s32[]{:T(128)}, f32[2,8]{0,1:T(8,128)S(1)}, f32[2,2,8,160,160]{4,3,1,0,2:T(8,128)}, /*index...) while((s32[]{:T(128)}, f32[2,2,160,160]{3,2,1,0:T(8,128)S(1)}, s32[]{:T(128)}, ...), condition=%wide.region_5.7_spmd, body=%wide.region_4.6_spmd.sunk | while | flops 393420800 | bytes 3605663 | solution.py:29
  89.9 2.1 fusion.97
  104.5 2.1 fusion.97
  126.6 5.0 %gather_fusion = f32[16,2,160,160]{3,2,1,0:T(8,128)} fusion(f32[8,2,160,160]{3,2,1,0:T(8,128)} %all-gather.3.cloned.1.call-done, s32[1024]{0:T(1024)S(1)} %pad_clamp_fusion.1), kind=kCustom, calls=%fused_computation | custom fusion | bytes 6553664 | tf_op jit(solution)/shard_map/gather | solution.py:71
  131.7 39.5 %while.40 = (s32[]{:T(128)}, f32[2,2,160,160]{3,2,1,0:T(8,128)S(1)}, s32[]{:T(128)}, f32[2,8]{0,1:T(8,128)S(1)}, f32[2,2,8,160,160]{4,3,1,0,2:T(8,128)}, /*index...) while((s32[]{:T(128)}, f32[2,2,160,160]{3,2,1,0:T(8,128)S(1)}, s32[]{:T(128)}, ...), condition=%wide.region_2.3_spmd, body=%wide.region_1.2_spmd.sunk | while | flops 393420800 | bytes 3605663 | solution.py:29
  134.5 2.1 fusion.91
  149.1 2.1 fusion.91
  153.9 2.1 fusion.91
  171.6 24.5 %collective-permute-done.2 = f32[2,2,160,160]{3,2,1,0:T(8,128)S(1)} collective-permute-done((f32[2,2,160,160]{3,2,1,0:T(8,128)S(1)}, f32[2,2,160,160]{3,2,1,0:T(8,128)S(1)}, u32[]{:S(2)}, u32[]{:S(2)}) %collective-permute-start.2) | collective-permute-done | bytes 409632 | tf_op jit(solution)/shard_map/ppermute | solution.py:66
  197.2 38.2 %collective-permute-done.3 = f32[2,4,160,160]{3,2,1,0:T(8,128)} collective-permute-done((f32[2,4,160,160]{3,2,1,0:T(8,128)S(1)}, f32[2,4,160,160]{3,2,1,0:T(8,128)}, u32[]{:S(2)}, u32[]{:S(2)}) %collective-permute-start.3) | collective-permute-done | bytes 819232 | tf_op jit(solution)/shard_map/ppermute | solution.py:66
  235.3 3.2 fusion.44
  238.5 3.1 gather_fusion.3
  241.6 5.4 %copy.59 = f32[2,8,2,160,160]{4,3,0,2,1:T(8,128)} copy(f32[2,8,2,160,160]{4,3,2,1,0:T(8,128)} %bitcast.100) | data formatting | bytes 6553600 | tf_op jit(solution)/shard_map/gather | solution.py:72
  247.1 39.5 %while.43 = (s32[]{:T(128)}, f32[2,2,160,160]{3,2,1,0:T(8,128)S(1)}, s32[]{:T(128)}, f32[2,8]{0,1:T(8,128)S(1)}, f32[2,2,8,160,160]{4,3,1,0,2:T(8,128)}, /*index...) while((s32[]{:T(128)}, f32[2,2,160,160]{3,2,1,0:T(8,128)S(1)}, s32[]{:T(128)}, ...), condition=%wide.region_9.11_spmd, body=%wide.region_8.10_spmd.sunk | while | flops 393420800 | bytes 3605663 | solution.py:29
  286.7 5.0 %gather_fusion.2 = f32[16,2,160,160]{3,2,1,0:T(8,128)} fusion(f32[8,2,160,160]{3,2,1,0:T(8,128)} %all-gather.5.cloned.1.call-done, s32[1024]{0:T(1024)S(1)} %pad_clamp_fusion.1), kind=kCustom, calls=%fused_computation.2 | custom fusion | bytes 6553664 | tf_op jit(solution)/shard_map/gather | solution.py:71
  291.6 5.4 %copy.60 = f32[2,8,2,160,160]{4,3,2,0,1:T(8,128)} copy(f32[2,8,2,160,160]{4,3,2,1,0:T(8,128)} %bitcast.101) | data formatting | bytes 6553600 | tf_op jit(solution)/shard_map/gather | solution.py:71
  297.1 39.5 %while.42 = (s32[]{:T(128)}, f32[2,2,160,160]{3,2,1,0:T(8,128)S(1)}, s32[]{:T(128)}, f32[2,8]{0,1:T(8,128)S(1)}, f32[2,2,8,160,160]{4,3,1,0,2:T(8,128)}, /*index...) while((s32[]{:T(128)}, f32[2,2,160,160]{3,2,1,0:T(8,128)S(1)}, s32[]{:T(128)}, ...), condition=%wide.region_7.9_spmd, body=%wide.region_6.8_spmd.sunk | while | flops 393420800 | bytes 3605663 | solution.py:29
  304.8 2.1 fusion.104
  (141 shorter events, 132.2 us)
Async XLA Ops:
  7.2 119.4 %all-gather.3.cloned.1.call-start = ((), (), s32[]{:S(2)}) async-start(), calls=%async_computation | async-start | bytes 3276800 | tf_op jit(solution)/shard_map/all_gather | solution.py:61
  7.2 16.0 %collective-permute-start = (f32[2,2,160,160]{3,2,1,0:T(8,128)}, f32[2,2,160,160]{3,2,1,0:T(8,128)S(1)}, u32[]{:S(2)}, u32[]{:S(2)}) collective-permute-start(f32[2,2,160,160]{3,2,1,0:T(8,128)} %param.23), channel_id=1, source_target_pairs={{0,3},{1,0},{2,1},{3,2},{4,7},{5,4},{6,5},{7,6},{8,11},{9,8},{10,9... | collective-permute-start | bytes 1228808 | tf_op jit(solution)/shard_map/ppermute | solution.py:66
  7.9 278.8 %all-gather.5.cloned.1.call-start = ((), (), s32[]{:S(2)}) async-start(), calls=%async_computation.1 | async-start | bytes 3276800 | tf_op jit(solution)/shard_map/all_gather | solution.py:61
  23.2 14.4 %copy-start.6 = (f32[2,2,160,160]{3,2,1,0:T(8,128)}, f32[2,2,160,160]{3,2,1,0:T(8,128)S(1)}, u32[]{:S(2)}) copy-start(f32[2,2,160,160]{3,2,1,0:T(8,128)S(1)} %collective-permute-done) | copy-start | bytes 1228804
  24.6 56.3 %collective-permute-start.1 = (f32[2,4,160,160]{3,2,1,0:T(8,128)S(1)}, f32[2,4,160,160]{3,2,1,0:T(8,128)}, u32[]{:S(2)}, u32[]{:S(2)}) collective-permute-start(f32[2,4,160,160]{3,2,1,0:T(8,128)S(1)} %pad_maximum_fusion), channel_id=1, source_target_pairs={{0,2},{1,3},{2,0},{3,1},{4,6},{5,7},{6,4},{7,5},{8,10},{9,11},{10,... | collective-permute-start | bytes 2457608 | tf_op jit(solution)/shard_map/ppermute | solution.py:66
  37.7 43.2 %copy-start.2 = (f32[2,2,160,160]{3,2,1,0:T(8,128)S(1)}, f32[2,2,160,160]{3,2,1,0:T(8,128)}, u32[]{:S(2)}) copy-start(f32[2,2,160,160]{3,2,1,0:T(8,128)} %param.23) | copy-start | bytes 1228804
  131.6 39.6 %copy-start.3 = (f32[2,2,160,160]{3,2,1,0:T(8,128)S(1)}, f32[2,2,160,160]{3,2,1,0:T(8,128)}, u32[]{:S(2)}) copy-start(f32[2,2,160,160]{3,2,1,0:T(8,128)} %param.23) | copy-start | bytes 1228804
  131.6 39.6 %copy-start.4 = (f32[2,2,160,160]{3,2,1,0:T(8,128)S(1)}, f32[2,2,160,160]{3,2,1,0:T(8,128)}, u32[]{:S(2)}) copy-start(f32[2,2,160,160]{3,2,1,0:T(8,128)} %param.24) | copy-start | bytes 1228804
  131.6 39.6 %copy-start.8 = (f32[2,2,160]{2,1,0:T(2,128)S(1)}, f32[2,2,160]{2,1,0:T(2,128)}, u32[]{:S(2)}) copy-start(f32[2,2,160]{2,1,0:T(2,128)} %param.33) | copy-start | bytes 7684
  131.6 39.6 %copy-start.9 = (f32[2]{0:T(128)S(1)}, f32[2]{0:T(128)}, u32[]{:S(2)}) copy-start(f32[2]{0:T(128)} %param.35) | copy-start | bytes 28
  131.7 39.6 %copy-start.10 = (f32[2]{0:T(128)S(1)}, f32[2]{0:T(128)}, u32[]{:S(2)}) copy-start(f32[2]{0:T(128)} %param.34) | copy-start | bytes 28
  171.6 25.6 %copy-start = (f32[2,2,160,160]{3,2,1,0:T(8,128)}, f32[2,2,160,160]{3,2,1,0:T(8,128)S(1)}, u32[]{:S(2)}) copy-start(f32[2,2,160,160]{3,2,1,0:T(8,128)S(1)} %divide_subtract_fusion.1) | copy-start | bytes 1228804
  171.6 24.5 %collective-permute-start.2 = (f32[2,2,160,160]{3,2,1,0:T(8,128)S(1)}, f32[2,2,160,160]{3,2,1,0:T(8,128)S(1)}, u32[]{:S(2)}, u32[]{:S(2)}) collective-permute-start(f32[2,2,160,160]{3,2,1,0:T(8,128)S(1)} %divide_subtract_fusion.1), channel_id=1, source_target_pairs={{0,3},{1,0},{2,1},{3,2},{4,7},{5,4},{6,5},{7,6},{8,11},{9,8},{10,9... | collective-permute-start | bytes 1228808 | tf_op jit(solution)/shard_map/ppermute | solution.py:66
  196.1 0.8 copy-start.7
  197.0 38.3 %collective-permute-start.3 = (f32[2,4,160,160]{3,2,1,0:T(8,128)S(1)}, f32[2,4,160,160]{3,2,1,0:T(8,128)}, u32[]{:S(2)}, u32[]{:S(2)}) collective-permute-start(f32[2,4,160,160]{3,2,1,0:T(8,128)S(1)} %pad_maximum_fusion.1), channel_id=1, source_target_pairs={{0,2},{1,3},{2,0},{3,1},{4,6},{5,7},{6,4},{7,5},{8,10},{9,11},{10,... | collective-permute-start | bytes 2457608 | tf_op jit(solution)/shard_map/ppermute | solution.py:66
  297.1 39.6 %copy-start.1 = (f32[2,2,160,160]{3,2,1,0:T(8,128)S(1)}, f32[2,2,160,160]{3,2,1,0:T(8,128)}, u32[]{:S(2)}) copy-start(f32[2,2,160,160]{3,2,1,0:T(8,128)} %copy-done) | copy-start | bytes 1228804
  297.1 39.6 %copy-start.5 = (f32[2,2,160,160]{3,2,1,0:T(8,128)S(1)}, f32[2,2,160,160]{3,2,1,0:T(8,128)}, u32[]{:S(2)}) copy-start(f32[2,2,160,160]{3,2,1,0:T(8,128)} %param.24) | copy-start | bytes 1228804
Sparse Core Ops, SparseCore 0:
  9.5 26.0 all-gather.2
  197.3 26.3 all-gather.4
